TPU v7x, 1024 devices: a whole 8x8x8 slice. The times are simulated.
1024 devices in a mesh: dp: 64 (over z_hi, y, core), tensor: 16 (over x, z_lo).
Axes of the slice: x: 8, y: 8, z: 8 (z_hi: 4, z_lo: 2; z = z_hi * 2 + z_lo), core: 2. Of those that a mesh axis runs over, the one named last changes fastest.
Arguments:
- activations: bfloat16 [131072, 4096], P(('dp', 'tensor')), may hold values from -24 to 24
- value_weight: bfloat16 [4096, 512], P('tensor'), may hold values from -0.09375 to 0.09375
- value_cotangent: bfloat16 [131072, 512], P(('dp', 'tensor')), may hold values from -6 to 6
Outputs:
- value_proj: bfloat16 [131072, 512], P(('dp', 'tensor'))
- input_grad: bfloat16 [131072, 4096], P(('dp', 'tensor'))
- weight_grad: float32 [4096, 512], P(('tensor', 'dp'))
All inputs are finite; a program needn't handle non-finite values.
Results may differ from a plain program's by a relative error of at most 0.001.
Values may be sent and summed in bfloat16 or wider, within the bound.
A program may use at most 32 MiB of HBM per device.

v0:
```python
import jax
import jax.numpy as jnp
from jax import lax
from jax.sharding import PartitionSpec as P


def per_device(activations, value_weight, value_cotangent):
    tok_rows = activations.shape[0]
    full_weight = lax.all_gather(value_weight, "tensor", axis=0, tiled=True)
    out_sum = jnp.dot(activations, full_weight, preferred_element_type=jnp.float32)
    grad_cols = lax.dot_general(
        value_cotangent, full_weight, (((1,), (1,)), ((), ())), preferred_element_type=jnp.float32
    )
    value_proj = out_sum.astype(jnp.bfloat16)
    input_grad = grad_cols.astype(jnp.bfloat16)
    own_columns = lax.all_to_all(activations, "tensor", split_axis=1, concat_axis=0, tiled=True)
    group_cot = lax.all_gather(value_cotangent, "tensor", axis=0, tiled=True)
    group_term = lax.dot_general(
        own_columns, group_cot, (((0,), (0,)), ((), ())), preferred_element_type=jnp.float32
    )
    summed = lax.psum_scatter(group_term, "dp", scatter_dimension=0, tiled=True)
    total_tokens = tok_rows * lax.axis_size("dp") * lax.axis_size("tensor")
    weight_grad = summed / jnp.sqrt(jnp.float32(total_tokens))
    return (value_proj, input_grad, weight_grad)


def solution(mesh):
    placed = (P(("dp", "tensor"), None), P("tensor", None), P(("dp", "tensor"), None))
    return jax.shard_map(
        per_device,
        mesh=mesh,
        in_specs=placed,
        out_specs=(P(("dp", "tensor"), None), P(("dp", "tensor"), None), P(("tensor", "dp"), None)),
        check_vma=False,
    )
```

profile of v0, /device:TPU:1, one launch (start us, length us, event | category | flops | bytes accessed | tf_op | source)
XLA Modules:
  0.0 792.6 jit_solution(236823941667884807)
XLA Ops:
  7.2 0.0 all-gather.5.cloned.1.call-start
  7.2 0.7 all-gather.5.cloned.1.call-update
  7.9 0.0 all-reduce.3.cloned.1.call-start
  7.9 1.6 copy.8
  9.6 0.0 copy-start.2
  9.6 30.8 %all_to_all.19 = bf16[128,16,256]{0,2,1:T(8,128)(2,1)S(1)} all-to-all(bf16[128,16,256]{0,2,1:T(8,128)(2,1)S(1)} %bitcast.11), channel_id=1, replica_groups=mesh['dp'=64,'tensor'=16] {'tensor'}, dimensions={1} | all-to-all | bytes 2097152 | tf_op jit(solution)/shard_map/all_to_all | solution.py:16
  40.4 0.5 copy.9
  40.9 52.5 %all-gather.5.cloned.1.call-done = bf16[2048,512]{1,0:T(8,128)(2,1)} async-done(((bf16[128,512]{1,0:T(8,128)(2,1)}), bf16[2048,512]{1,0:T(8,128)(2,1)}) %all-gather.5.cloned.1.call-update) | async-done | bytes 2097168 | tf_op jit(solution)/shard_map/all_gather | solution.py:17
  93.5 0.0 copy-start.1
  93.5 3.2 fusion
  96.7 0.0 all-reduce.3.cloned.1.call-update
  96.7 0.0 all-gather.3.cloned.1.call-start
  96.7 0.7 all-gather.3.cloned.1.call-update
  97.4 1.3 dynamic-slice
  99.3 578.5 %all-reduce.3.cloned.1.call-done = f32[256,512]{1,0:T(8,128)} async-done(((f32[256,512]{1,0:T(8,128)}), f32[256,512]{1,0:T(8,128)}) %all-reduce.3.cloned.1.call-update) | async-done | bytes 524304
  677.8 1.3 dynamic-slice_multiply_fusion
  679.1 100.8 %all-gather.3.cloned.1.call-done = bf16[4096,512]{1,0:T(8,128)(2,1)} async-done(((bf16[256,512]{1,0:T(8,128)(2,1)}), bf16[4096,512]{1,0:T(8,128)(2,1)}) %all-gather.3.cloned.1.call-update) | async-done | bytes 4194320 | tf_op jit(solution)/shard_map/all_gather | solution.py:9
  779.9 0.0 copy-done.2
  779.9 0.0 copy-start
  779.9 4.8 convolution_convert_fusion
  784.7 0.0 copy-done.1
  784.7 0.0 copy-done
  784.7 1.4 convolution_convert_fusion.1
Async XLA Ops:
  7.2 86.3 %all-gather.5.cloned.1.call-start = ((), (), s32[]{:S(2)}) async-start(), calls=%async_computation.2 | async-start | bytes 2228224 | tf_op jit(solution)/shard_map/all_gather | solution.py:17
  7.9 669.9 %all-reduce.3.cloned.1.call-start = ((), (), s32[]{:S(2)}) async-start(), calls=%async_computation.3 | async-start | bytes 1048576
  9.6 770.4 %copy-start.2 = (bf16[128,512]{1,0:T(8,128)(2,1)S(1)}, bf16[128,512]{1,0:T(8,128)(2,1)}, u32[]{:S(2)}) copy-start(bf16[128,512]{1,0:T(8,128)(2,1)} %param.5) | copy-start | bytes 393220
  93.5 691.3 %copy-start.1 = (bf16[128,4096]{1,0:T(8,128)(2,1)S(1)}, bf16[128,4096]{1,0:T(8,128)(2,1)}, u32[]{:S(2)}) copy-start(bf16[128,4096]{1,0:T(8,128)(2,1)} %param.3) | copy-start | bytes 3145732
  96.7 683.2 %all-gather.3.cloned.1.call-start = ((), (), s32[]{:S(2)}) async-start(), calls=%async_computation.1 | async-start | bytes 4456448 | tf_op jit(solution)/shard_map/all_gather | solution.py:9
  779.9 4.8 copy-start
Sparse Core Ops, SparseCore 0:
  10.6 82.7 all-gather.4
  97.5 580.2 all-reduce.2
  680.5 99.3 all-gather.2
where the time goes:
time: 794 us; the launch traced here: 793 us
  waiting for transfers between devices  733 us (92%)
  blocking collectives  30.8 us (4%)
  between operations  14.4 us (2%)
  matrix products  9.36 us (1%)
    unnamed x4, waiting for transfers between devices  580 us
    all_gather x1, waiting for transfers between devices, per_device(): full_weight = lax.all_gather(value_weight, 'tensor', axis=0, tiled=True)  101 us
    all_gather x1, waiting for transfers between devices, per_device(): group_cot = lax.all_gather(value_cotangent, 'tensor', axis=0, tiled=True)  52.5 us
    all_to_all x1, blocking collectives, per_device(): lax.all_to_all(activations, 'tensor', split_axis=1, concat_axis=0, tiled=...  30.8 us
  transfers between devices with their start and end apart: 3, of which 3 were waited for; matrix products, arithmetic and copies ran while one was open for 1% of the time, Pallas kernels for 0%

commit v1 on v0

v1 whole, which is shorter than its diff:
```python
import functools

import jax
import jax.numpy as jnp
from jax import lax
from jax.experimental import pallas as pl
from jax.experimental.pallas import tpu as pltpu
from jax.sharding import PartitionSpec as P

MESH = pl.DeviceIdType.MESH
RING = 8
ITEMS = 28


def _mod(v):
    return lax.rem(v + 4 * RING, RING)


def _kernel(scale, acts, w, cot, vp_out, ig_out, wg_out,
            a_all, c_pair, c_own, w_all, part, recv_r, recv_l, recv2_r, recv2_l, recv3_r, recv3_l,
            vp_acc, vp_buf, ig_buf, fin, fin_in, wg_buf,
            s_load, s_ax, r_ax, s_cx, r_cx, s_zx, r_zx,
            s_r, r_r, s_l, r_l, s_x, r_x, s_p, r_p,
            s2_r, r2_r, s2_l, r2_l, s3_r, r3_r, s3_l, r3_l, s_f, r_f, s_out):
    dp, tn = lax.axis_index("dp"), lax.axis_index("tensor")
    c, y, zh = lax.rem(dp, 2), lax.rem(lax.div(dp, 2), RING), lax.div(dp, 2 * RING)
    x, zl = lax.div(tn, 2), lax.rem(tn, 2)
    z = zh * 2 + zl
    oc = 1 - c
    sx = 1 - 2 * c
    pa = y * oc + z * c
    pb = z * oc + y * c

    def dev(xx, yy, zz, cc):
        return {"dp": lax.div(zz, 2) * (2 * RING) + yy * 2 + cc, "tensor": xx * 2 + lax.rem(zz, 2)}

    def along_a(step):
        return dev(x, _mod(y + step * oc), _mod(z + step * c), c)

    def along_b(step):
        return dev(x, _mod(y + step * c), _mod(z + step * oc), c)

    def along_x(step):
        return dev(_mod(x + step), y, z, c)

    partner = dev(x, y, z, oc)
    tok, cols = 128, 512

    loads = [
        pltpu.make_async_copy(acts, a_all.at[pl.ds(0, tok)], s_load.at[0]),
        pltpu.make_async_copy(cot.at[:, pl.ds(pl.multiple_of(c * 256, 256), 256)], c_pair.at[pl.ds(0, tok)], s_load.at[1]),
        pltpu.make_async_copy(cot, c_own, s_load.at[2]),
        pltpu.make_async_copy(w, w_all.at[x, pl.ds(zl * 4, 4)], s_load.at[3]),
    ]
    for load in loads:
        load.start()

    barrier = pltpu.get_barrier_semaphore()
    for there in (partner, along_a(1), along_a(-1), along_b(1), along_b(-1), along_x(1), along_x(-1)):
        pl.semaphore_signal(barrier, inc=1, device_id=there, device_id_type=MESH)
    pl.semaphore_wait(barrier, 7)

    def remote(src, dst, send, recv, there):
        return pltpu.make_async_remote_copy(
            src_ref=src, dst_ref=dst, send_sem=send, recv_sem=recv, device_id=there, device_id_type=MESH
        )

    def order(j):
        k = j // 2
        return 4 - k if j % 2 == 0 else k - 3

    def a_copy(j):
        block = pl.ds(pl.multiple_of(_mod(x + order(j)) * cols, cols), cols)
        return remote(acts.at[:, block], a_all.at[pl.ds(tok, tok), block], s_ax.at[j], r_ax.at[j], partner)

    c_copy = remote(cot.at[:, pl.ds(pl.multiple_of(oc * 256, 256), 256)], c_pair.at[pl.ds(tok, tok)], s_cx, r_cx, partner)
    c_copy.start()
    for j in range(8):
        a_copy(j).start()

    def unit(m):
        return lax.rem(zl + m // 4, 2) * 4 + lax.rem(m, 4)

    z_there = dev(x, y, _mod(z - sx), c)
    z_copy = remote(w, w_all.at[x, pl.ds(zl * 4, 4)], s_zx, r_zx, z_there)
    z_copy.start()
    z_wait = remote(w, w_all.at[x, pl.ds((1 - zl) * 4, 4)], s_zx, r_zx, z_there)

    x_there = along_x(sx)

    def x_place(i, m):
        return w_all.at[_mod(x - sx * (i // 8 + 1)), unit(m)]

    def x_in(i):
        m = lax.rem(i, 8) + lax.div(i, 24) * 4 * c
        return x_place(i, m)

    def x_recv(i):
        here = x_in(i)
        remote(here, here, s_x.at[i], r_x.at[i], x_there).wait_recv()
        remote(here, here, s_p.at[i], r_p.at[i], partner).start()

    def x_send(i, out):
        here = x_in(i)
        remote(here, here, s_x.at[out], r_x.at[out], x_there).start()

    def p_recv(i):
        m = lax.rem(i, 8) + lax.div(i, 24) * 4 * oc
        here = w_all.at[_mod(x + sx * (i // 8 + 1)), unit(m)]
        remote(here, here, s_p.at[i], r_p.at[i], partner).wait_recv()

    for m in range(4):
        here = w_all.at[x, unit(m)]
        remote(w.at[m], here, s_x.at[m], r_x.at[m], x_there).start()

    def weights_block(block, first=False):
        at = pl.ds(pl.multiple_of(block * cols, cols), cols)
        wb = w_all[block].reshape(cols, cols)
        term = jnp.dot(a_all[pl.ds(0, tok), at], wb, preferred_element_type=jnp.float32)
        if first:
            vp_acc[...] = term
        else:
            vp_acc[...] += term
        grad = lax.dot_general(c_own[...], wb, (((1,), (1,)), ((), ())), preferred_element_type=jnp.float32)
        ig_buf[:, at] = grad.astype(jnp.bfloat16)
        pltpu.make_async_copy(ig_buf.at[:, at], ig_out.at[:, at], s_out.at[block]).start()

    right, left = along_a(1), along_a(-1)

    def r_copy(n, to, xx):
        return remote(part.at[_mod(pa + to), _mod(x + xx)], recv_r.at[n], s_r.at[n], r_r.at[n], right)

    def l_copy(n, to, xx):
        return remote(part.at[_mod(pa - to), _mod(x + xx)], recv_l.at[n], s_l.at[n], r_l.at[n], left)

    for load in loads[:3]:
        load.wait()
    c_copy.wait_recv()
    for j in range(8):
        k = j // 2
        a_copy(j).wait_recv()
        xb = _mod(x + order(j))
        at = pl.ds(pl.multiple_of(xb * cols, cols), cols)
        prod = lax.dot_general(
            a_all[:, at], c_pair[...], (((0,), (0,)), ((), ())), preferred_element_type=jnp.float32
        )
        for zz in range(8):
            base = (zz % 2) * 256 + (zz // 2) * 64
            for yy in range(8):
                part[yy * oc + zz * c, xb, zz * oc + yy * c] = prod[base + yy * 8 : base + yy * 8 + 8]
        if j % 2 == 0:
            r_copy(2 * k, 4, order(j)).start()
            l_copy(2 * k + 1, 3, order(j)).start()
        else:
            r_copy(2 * k + 1, 3, order(j)).start()
            l_copy(2 * k, 4, order(j)).start()

    loads[3].wait()
    z_wait.wait_recv()
    for m in range(4, 8):
        here = w_all.at[x, unit(m)]
        remote(here, here, s_x.at[m], r_x.at[m], x_there).start()
    weights_block(x, first=True)

    def pass_on(i, n_out):
        x_recv(i)
        x_send(i, n_out)

    lax.fori_loop(0, 8, lambda i, u: (pass_on(i, i + 8), u)[1], 0)

    def ring_step(p, k):
        n_even, n_odd = 8 * (p - 1) + 2 * k, 8 * (p - 1) + 2 * k + 1
        e_r, e_l = 4 - k, k - 3
        r_copy(n_even, 0, 0).wait_recv()
        part[_mod(pa + 4 - p), _mod(x + e_r)] += recv_r[n_even]
        l_copy(n_even, 0, 0).wait_recv()
        part[_mod(pa - 4 + p), _mod(x + e_l)] += recv_l[n_even]
        r_copy(n_odd, 0, 0).wait_recv()
        part[_mod(pa + 3 - p), _mod(x + e_l)] += recv_r[n_odd]
        l_copy(n_odd, 0, 0).wait_recv()
        part[_mod(pa - 3 + p), _mod(x + e_r)] += recv_l[n_odd]
        if p < 3:
            r_copy(8 * p + 2 * k, 4 - p, e_r).start()
            l_copy(8 * p + 2 * k, 4 - p, e_l).start()
            r_copy(8 * p + 2 * k + 1, 3 - p, e_l).start()
            l_copy(8 * p + 2 * k + 1, 3 - p, e_r).start()
        else:
            r_copy(24 + k, 1, e_r).start()
            l_copy(24 + k, 1, e_l).start()

    def p_block(p):
        lax.fori_loop(8 * p - 8, 8 * p, lambda i, u: (p_recv(i), u)[1], 0)
        weights_block(_mod(x + sx * p))

    for p in (1, 2, 3):

        def tick(k, u, p=p):
            ring_step(p, k)
            for h in range(2):
                i = 8 * p + 2 * k + h
                if p == 1:
                    pass_on(i, i + 8)
                elif p == 2:
                    x_recv(i)

                    @pl.when((1 - lax.div(k, 2)) * oc + lax.div(k, 2) * c == 1)
                    def _():
                        x_send(i, 24 + lax.rem(i, 4))
            if p == 3:
                x_recv(24 + k)
            return u

        lax.fori_loop(0, 2, tick, 0)
        weights_block(_mod(x - sx * p))
        lax.fori_loop(2, 4, tick, 0)
        p_block(p)

    x_right, x_left = along_x(1), along_x(-1)

    def half2(ref, h):
        return ref.at[pl.ds(h * 4, 4)]

    def r2_copy(n):
        src = half2(part.at[pa, _mod(x + 4 - (n + 1) // 2)], n % 2)
        return remote(src, recv2_r.at[n], s2_r.at[n], r2_r.at[n], x_right)

    def l2_copy(n):
        src = half2(part.at[pa, _mod(x - 4 + (n + 1) // 2)], (n + 1) % 2)
        return remote(src, recv2_l.at[n], s2_l.at[n], r2_l.at[n], x_left)

    for k in range(4):
        r_copy(24 + k, 0, 0).wait_recv()
        part[pa, _mod(x + 4 - k)] += recv_r[24 + k]
        l_copy(24 + k, 0, 0).wait_recv()
        part[pa, _mod(x + k - 3)] += recv_l[24 + k]
        if k < 2:
            r2_copy(k).start()
            l2_copy(k).start()

    def last_block():
        lax.fori_loop(24, 28, lambda i, u: (p_recv(i), u)[1], 0)
        weights_block(_mod(x + 4))
        vp_buf[...] = vp_acc[...].astype(jnp.bfloat16)
        pltpu.make_async_copy(vp_buf, vp_out, s_out.at[8]).start()

    last_block()
    for n in range(7):
        to = 4 - (n + 1) // 2 - 1
        r2_copy(n).wait_recv()
        mine = half2(part.at[pa, _mod(x + to)], n % 2)
        mine[...] += recv2_r[n]
        l2_copy(n).wait_recv()
        mine = half2(part.at[pa, _mod(x - to)], (n + 1) % 2)
        mine[...] += recv2_l[n]
        if n + 2 < 7:
            r2_copy(n + 2).start()
            l2_copy(n + 2).start()

    b_right, b_left = along_b(1), along_b(-1)

    def r3_copy(n):
        return remote(part.at[pa, x, _mod(pb + 4 - n)], recv3_r.at[n], s3_r.at[n], r3_r.at[n], b_right)

    def l3_copy(n):
        return remote(part.at[pa, x, _mod(pb - 3 + n)], recv3_l.at[n], s3_l.at[n], r3_l.at[n], b_left)

    r3_copy(0).start()
    l3_copy(0).start()
    for n in range(4):
        if n < 3:
            l3_copy(n).wait_recv()
            part[pa, x, _mod(pb - 2 + n)] += recv3_l[n]
        if n < 2:
            l3_copy(n + 1).start()
        r3_copy(n).wait_recv()
        part[pa, x, _mod(pb + 3 - n)] += recv3_r[n]
        if n < 3:
            r3_copy(n + 1).start()

    total = part[pa, x, pb] / scale
    fin[...] = jnp.where(c == 0, total[4:], total[:4])
    f_copy = remote(fin, fin_in, s_f, r_f, partner)
    f_copy.start()
    stay = jnp.where(c == 0, total[:4], total[4:])
    f_copy.wait_recv()
    other = fin_in[...]
    wg_buf[:, :256] = jnp.where(c == 0, stay, other)
    wg_buf[:, 256:] = jnp.where(c == 0, other, stay)
    wg_copy = pltpu.make_async_copy(wg_buf, wg_out, s_out.at[9])
    wg_copy.start()

    c_copy.wait_send()
    z_copy.wait_send()
    f_copy.wait_send()
    for j in range(8):
        a_copy(j).wait_send()

    def sent(n, u):
        r_copy(n, 0, 0).wait_send()
        l_copy(n, 0, 0).wait_send()
        here = w_all.at[0, 0]
        remote(here, here, s_x.at[n], r_x.at[n], x_there).wait_send()
        remote(here, here, s_p.at[n], r_p.at[n], partner).wait_send()
        return u

    lax.fori_loop(0, ITEMS, sent, 0)
    for n in range(7):
        r2_copy(n).wait_send()
        l2_copy(n).wait_send()
    for n in range(4):
        r3_copy(n).wait_send()
    for n in range(3):
        l3_copy(n).wait_send()
    for b in range(8):
        at = pl.ds(b * cols, cols)
        pltpu.make_async_copy(ig_buf.at[:, at], ig_out.at[:, at], s_out.at[b]).wait()
    pltpu.make_async_copy(vp_buf, vp_out, s_out.at[8]).wait()
    wg_copy.wait()


def per_device(activations, value_weight, value_cotangent):
    tok, d = activations.shape
    rows, v = value_weight.shape
    tokens = tok * lax.axis_size("dp") * lax.axis_size("tensor")
    f32, bf16 = jnp.float32, jnp.bfloat16
    dma, vm = pltpu.SemaphoreType.DMA, pltpu.VMEM
    hbm = pl.BlockSpec(memory_space=pl.ANY)
    return pl.pallas_call(
        functools.partial(_kernel, float(tokens) ** 0.5),
        out_shape=(
            jax.ShapeDtypeStruct((tok, v), bf16),
            jax.ShapeDtypeStruct((tok, d), bf16),
            jax.ShapeDtypeStruct((rows * lax.axis_size("tensor") // 1024, v), f32),
        ),
        in_specs=[hbm] * 3,
        out_specs=(hbm,) * 3,
        scratch_shapes=[
            vm((256, 4096), bf16), vm((256, 256), bf16), vm((128, 512), bf16), vm((8, 8, 64, 512), bf16),
            vm((8, 8, 8, 8, 256), f32), vm((ITEMS, 8, 8, 256), f32), vm((ITEMS, 8, 8, 256), f32),
            vm((7, 4, 8, 256), f32), vm((7, 4, 8, 256), f32), vm((4, 8, 256), f32), vm((3, 8, 256), f32),
            vm((128, 512), f32), vm((128, 512), bf16), vm((128, 4096), bf16),
            vm((4, 256), f32), vm((4, 256), f32), vm((4, 512), f32),
            dma((4,)), dma((8,)), dma((8,)), dma, dma, dma, dma,
            dma((ITEMS,)), dma((ITEMS,)), dma((ITEMS,)), dma((ITEMS,)),
            dma((ITEMS,)), dma((ITEMS,)), dma((ITEMS,)), dma((ITEMS,)),
            dma((7,)), dma((7,)), dma((7,)), dma((7,)), dma((4,)), dma((4,)), dma((3,)), dma((3,)),
            dma, dma, dma((10,)),
        ],
        compiler_params=pltpu.CompilerParams(
            collective_id=0, has_side_effects=True, vmem_limit_bytes=48 * 1024 * 1024
        ),
    )(activations, value_weight.reshape(4, 64, v), value_cotangent)


def solution(mesh):
    placed = (P(("dp", "tensor"), None), P("tensor", None), P(("dp", "tensor"), None))
    return jax.shard_map(
        per_device,
        mesh=mesh,
        in_specs=placed,
        out_specs=(P(("dp", "tensor"), None), P(("dp", "tensor"), None), P(("tensor", "dp"), None)),
        check_vma=False,
    )
```

time: 794 us -> 86.1 us (0.11)
  waiting for transfers between devices: 733 us -> 0 us
  Pallas kernels: 0 us -> 79.9 us
  blocking collectives: 30.8 us -> 0 us
  between operations: 14.4 us -> 0.65 us
  matrix products: 9.36 us -> 0 us
    unnamed x4 -> x0, waiting for transfers between devices: 580 us -> none
    all_gather x2 -> x0, waiting for transfers between devices: 153 us -> none  [the longest x1 101 us: per_device(): full_weight = lax.all_gather(value_weight, 'tensor', axis=0, tiled=True)]
    pallas_call x0 -> x1, Pallas kernels: none -> 79.9 us  [per_device(): pl.pallas_call(functools.partial(_kernel, float(tokens) ** 0.5), out_shap...]
    all_to_all x1 -> x0, blocking collectives: 30.8 us -> none  [per_device(): lax.all_to_all(activations, 'tensor', split_axis=1, concat_axis=0, tiled=...]
    dot_general x3 -> x0, matrix products: 9.36 us -> none  [the longest x1 4.78 us: per_device(): lax.dot_general(value_cotangent, full_weight, (((1,), (1,)), ((), ())), p...]
  transfers between devices with their start and end apart: 3 -> 0, of which waited for: 3 -> 0; matrix products, arithmetic and copies ran while one was open for 1% -> 0% of each run, Pallas kernels for 0% -> 0%
where the time goes in v1:
time: 86.1 us; the launch traced here: 85.8 us
  Pallas kernels  79.9 us (93%)
  local copies, waits for them, and re-layouts  5.3 us (6%)
    pallas_call x1, Pallas kernels, per_device(): pl.pallas_call(functools.partial(_kernel, float(tokens) ** 0.5), out_shap...  79.9 us
    unnamed x9, local copies, waits for them, and re-layouts  5.3 us

profile of v1, /device:TPU:1, one launch (start us, length us, event | category | flops | bytes accessed | tf_op | source)
XLA Modules:
  0.0 85.8 jit_solution(11479805568969029898)
XLA Ops:
  0.6 0.0 copy-start
  0.6 1.2 %copy-done = bf16[128,4096]{1,0:T(8,128)(2,1)S(1)} copy-done((bf16[128,4096]{1,0:T(8,128)(2,1)S(1)}, bf16[128,4096]{1,0:T(8,128)(2,1)}, u32[]{:S(2)}) %copy-start) | copy-done | bytes 1048600
  1.9 0.0 copy-start.1
  1.9 0.9 %copy-done.1 = bf16[256,512]{1,0:T(8,128)(2,1)S(1)} copy-done((bf16[256,512]{1,0:T(8,128)(2,1)S(1)}, bf16[256,512]{1,0:T(8,128)(2,1)}, u32[]{:S(2)}) %copy-start.1) | copy-done | bytes 262168
  2.8 0.0 copy-start.2
  2.8 0.9 %copy-done.2 = bf16[128,512]{1,0:T(8,128)(2,1)S(1)} copy-done((bf16[128,512]{1,0:T(8,128)(2,1)S(1)}, bf16[128,512]{1,0:T(8,128)(2,1)}, u32[]{:S(2)}) %copy-start.2) | copy-done | bytes 131096
  3.7 79.9 %shard_map.58 = (bf16[128,512]{1,0:T(8,128)(2,1)S(1)}, bf16[128,4096]{1,0:T(8,128)(2,1)S(1)}, f32[4,512]{1,0:T(4,128)S(1)}) custom-call(bf16[128,4096]{1,0:T(8,128)(2,1)S(1)} %copy-done, bf16[4,64,512]{2,1,0:T(8,128)(2,1)S(1)} %bitcast.1, bf16[128,512]{1,0:T(8,128)(2,1)S(1)} %copy-done.2), custom_call_target="tpu_custom_call" | custom-call | tf_op jit(solution)/shard_map/pallas_call | solution.py:328
  83.6 0.7 copy.9
  84.3 1.0 %copy.10 = bf16[128,4096]{1,0:T(8,128)(2,1)} copy(bf16[128,4096]{1,0:T(8,128)(2,1)S(1)} %get-tuple-element.7) | data formatting | bytes 2097152
  85.3 0.6 copy.11
Async XLA Ops:
  0.6 1.2 %copy-start = (bf16[128,4096]{1,0:T(8,128)(2,1)S(1)}, bf16[128,4096]{1,0:T(8,128)(2,1)}, u32[]{:S(2)}) copy-start(bf16[128,4096]{1,0:T(8,128)(2,1)} %acts.1) | copy-start | bytes 3145732
  1.9 0.9 %copy-start.1 = (bf16[256,512]{1,0:T(8,128)(2,1)S(1)}, bf16[256,512]{1,0:T(8,128)(2,1)}, u32[]{:S(2)}) copy-start(bf16[256,512]{1,0:T(8,128)(2,1)} %param.4) | copy-start | bytes 786436
  2.8 0.9 %copy-start.2 = (bf16[128,512]{1,0:T(8,128)(2,1)S(1)}, bf16[128,512]{1,0:T(8,128)(2,1)}, u32[]{:S(2)}) copy-start(bf16[128,512]{1,0:T(8,128)(2,1)} %cot.1) | copy-start | bytes 393220

commit v2 on v1

v2 whole, which is shorter than its diff:
```python
import functools

import jax
import jax.numpy as jnp
from jax import lax
from jax.experimental import pallas as pl
from jax.experimental.pallas import tpu as pltpu
from jax.sharding import PartitionSpec as P

MESH = pl.DeviceIdType.MESH
RING = 8
ITEMS = 28


def _mod(v):
    return lax.rem(v + 4 * RING, RING)


def _kernel(scale, acts, w, cot, vp_out, ig_out, wg_out,
            a_all, c_pair, c_own, w_all, part, recv_r, recv_l, recv2, s2_buf, recv3,
            vp_acc, vp_buf, ig_buf, wg_buf,
            s_load, s_ax, r_ax, s_cx, r_cx, s_zx, r_zx, s_zp, r_zp,
            s_r, r_r, s_l, r_l, s_x, r_x, s_p, r_p, s_2, r_2, s_3, r_3, s_out):
    dp, tn = lax.axis_index("dp"), lax.axis_index("tensor")
    c, y, zh = lax.rem(dp, 2), lax.rem(lax.div(dp, 2), RING), lax.div(dp, 2 * RING)
    x, zl = lax.div(tn, 2), lax.rem(tn, 2)
    z = zh * 2 + zl
    oc = 1 - c
    sx = 1 - 2 * c
    pa = y * oc + z * c
    pb = z * oc + y * c

    def dev(xx, yy, zz, cc):
        return {"dp": lax.div(zz, 2) * (2 * RING) + yy * 2 + cc, "tensor": xx * 2 + lax.rem(zz, 2)}

    def along_a(step):
        return dev(x, _mod(y + step * oc), _mod(z + step * c), c)

    def along_b(step):
        return dev(x, _mod(y + step * c), _mod(z + step * oc), c)

    def along_x(step):
        return dev(_mod(x + step), y, z, c)

    partner = dev(x, y, z, oc)
    tok, cols = 128, 512

    barrier = pltpu.get_barrier_semaphore()
    for there in (partner, along_a(1), along_a(-1), along_b(1), along_b(-1), along_x(1), along_x(-1)):
        pl.semaphore_signal(barrier, inc=1, device_id=there, device_id_type=MESH)

    loads = [
        pltpu.make_async_copy(acts, a_all.at[pl.ds(0, tok)], s_load.at[0]),
        pltpu.make_async_copy(cot.at[:, pl.ds(pl.multiple_of(c * 256, 256), 256)], c_pair.at[pl.ds(0, tok)], s_load.at[1]),
        pltpu.make_async_copy(cot, c_own, s_load.at[2]),
        pltpu.make_async_copy(w, w_all.at[x, pl.ds(zl * 4, 4)], s_load.at[3]),
    ]
    for load in loads:
        load.start()
    pl.semaphore_wait(barrier, 7)

    def remote(src, dst, send, recv, there):
        return pltpu.make_async_remote_copy(
            src_ref=src, dst_ref=dst, send_sem=send, recv_sem=recv, device_id=there, device_id_type=MESH
        )

    z_there = dev(x, y, _mod(z - sx), c)
    z_copy = remote(w.at[pl.ds(2 * c, 2)], w_all.at[x, pl.ds(zl * 4 + 2 * c, 2)], s_zx, r_zx, z_there)
    z_copy.start()
    z_mine = w_all.at[x, pl.ds((1 - zl) * 4 + 2 * c, 2)]
    z_other = w_all.at[x, pl.ds((1 - zl) * 4 + 2 * oc, 2)]

    def order(j):
        k = j // 2
        return 4 - k if j % 2 == 0 else k - 3

    def a_copy(j):
        block = pl.ds(pl.multiple_of(_mod(x + order(j)) * cols, cols), cols)
        return remote(acts.at[:, block], a_all.at[pl.ds(tok, tok), block], s_ax, r_ax.at[j], partner)

    c_copy = remote(cot.at[:, pl.ds(pl.multiple_of(oc * 256, 256), 256)], c_pair.at[pl.ds(tok, tok)], s_cx, r_cx, partner)
    c_copy.start()
    for j in range(8):
        a_copy(j).start()

    def unit(m):
        return lax.rem(zl + m // 4, 2) * 4 + lax.rem(m, 4)

    x_there = along_x(sx)

    def x_in(i):
        m = lax.rem(i, 8) + lax.div(i, 24) * 4 * c
        return w_all.at[_mod(x - sx * (i // 8 + 1)), unit(m)]

    def x_recv(i):
        here = x_in(i)
        remote(here, here, s_x, r_x.at[i], x_there).wait_recv()
        remote(here, here, s_p, r_p.at[i // 8], partner).start()

    def x_send(i, out):
        here = x_in(i)
        remote(here, here, s_x, r_x.at[out], x_there).start()

    def x_own(m):
        here = w_all.at[x, unit(m)]
        remote(here, here, s_x, r_x.at[m], x_there).start()

    for m in range(4):
        remote(w.at[m], w_all.at[x, unit(m)], s_x, r_x.at[m], x_there).start()

    def weights_block(block, first=False):
        at = pl.ds(pl.multiple_of(block * cols, cols), cols)
        wb = w_all[block].reshape(cols, cols)
        term = jnp.dot(a_all[pl.ds(0, tok), at], wb, preferred_element_type=jnp.float32)
        if first:
            vp_acc[...] = term
        else:
            vp_acc[...] += term
        grad = lax.dot_general(c_own[...], wb, (((1,), (1,)), ((), ())), preferred_element_type=jnp.float32)
        ig_buf[:, at] = grad.astype(jnp.bfloat16)
        pltpu.make_async_copy(ig_buf.at[:, at], ig_out.at[:, at], s_out.at[block]).start()

    def partner_block(p):
        whole = w_all.at[0] if p < 4 else w_all.at[0, pl.ds(0, 4)]
        remote(whole, whole, s_p, r_p.at[p - 1], partner).wait_recv()
        if p < 4:
            weights_block(_mod(x + sx * p))

    right, left = along_a(1), along_a(-1)

    def r_copy(n, to, xx):
        return remote(part.at[_mod(pa + to), _mod(x + xx)], recv_r.at[n], s_r, r_r.at[n], right)

    def l_copy(n, to, xx):
        return remote(part.at[_mod(pa - to), _mod(x + xx)], recv_l.at[n], s_l, r_l.at[n], left)

    for load in loads[:3]:
        load.wait()
    c_copy.wait_recv()
    for j in range(8):
        k = j // 2
        a_copy(j).wait_recv()
        xb = _mod(x + order(j))
        at = pl.ds(pl.multiple_of(xb * cols, cols), cols)
        prod = lax.dot_general(
            a_all[:, at], c_pair[...], (((0,), (0,)), ((), ())), preferred_element_type=jnp.float32
        )
        for zz in range(8):
            base = (zz % 2) * 256 + (zz // 2) * 64
            for yy in range(8):
                part[yy * oc + zz * c, xb, zz * oc + yy * c] = prod[base + yy * 8 : base + yy * 8 + 8]
        if j % 2 == 0:
            r_copy(2 * k, 4, order(j)).start()
            l_copy(2 * k + 1, 3, order(j)).start()
        else:
            r_copy(2 * k + 1, 3, order(j)).start()
            l_copy(2 * k, 4, order(j)).start()

    def ring_step(p, k):
        n_even, n_odd = 8 * (p - 1) + 2 * k, 8 * (p - 1) + 2 * k + 1
        e_r, e_l = 4 - k, k - 3
        r_copy(n_even, 0, 0).wait_recv()
        part[_mod(pa + 4 - p), _mod(x + e_r)] += recv_r[n_even]
        l_copy(n_even, 0, 0).wait_recv()
        part[_mod(pa - 4 + p), _mod(x + e_l)] += recv_l[n_even]
        r_copy(n_odd, 0, 0).wait_recv()
        part[_mod(pa + 3 - p), _mod(x + e_l)] += recv_r[n_odd]
        l_copy(n_odd, 0, 0).wait_recv()
        part[_mod(pa - 3 + p), _mod(x + e_r)] += recv_l[n_odd]
        if p < 3:
            r_copy(8 * p + 2 * k, 4 - p, e_r).start()
            l_copy(8 * p + 2 * k, 4 - p, e_l).start()
            r_copy(8 * p + 2 * k + 1, 3 - p, e_l).start()
            l_copy(8 * p + 2 * k + 1, 3 - p, e_r).start()
        else:
            r_copy(24 + k, 1, e_r).start()
            l_copy(24 + k, 1, e_l).start()

    def tick(p, forward):
        def body(k, u):
            ring_step(p, k)
            if forward is not None:
                for h in range(2):
                    i = 8 * p - 12 + 2 * k + h
                    x_recv(i)
                    forward(i)
            return u

        return body

    def forward(i):
        x_send(i, i + 8)

    def forward_last(i):
        @pl.when(c == lax.div(i - 16, 4))
        def _():
            x_send(i, 24 + lax.rem(i, 4))

    lax.fori_loop(0, 1, tick(1, None), 0)
    remote(z_mine, z_mine, s_zx, r_zx, z_there).wait_recv()
    remote(z_mine, z_mine, s_zp, r_zp, partner).start()
    x_own(4 + 2 * c)
    x_own(5 + 2 * c)
    lax.fori_loop(1, 2, tick(1, None), 0)
    remote(z_other, z_other, s_zp, r_zp, partner).wait_recv()
    x_own(4 + 2 * oc)
    x_own(5 + 2 * oc)
    lax.fori_loop(2, 4, tick(1, forward), 0)
    loads[3].wait()
    weights_block(x, first=True)
    lax.fori_loop(0, 2, tick(2, forward), 0)
    weights_block(_mod(x - sx))
    lax.fori_loop(2, 4, tick(2, forward), 0)
    partner_block(1)
    lax.fori_loop(0, 2, tick(3, forward), 0)
    weights_block(_mod(x - 2 * sx))
    lax.fori_loop(2, 4, tick(3, forward_last), 0)
    partner_block(2)

    far_first = (4, 3, 5, 2, 6, 1, 7)

    def last_step(k, u):
        r_copy(24 + k, 0, 0).wait_recv()
        part[pa, _mod(x + 4 - k)] += recv_r[24 + k]
        l_copy(24 + k, 0, 0).wait_recv()
        part[pa, _mod(x + k - 3)] += recv_l[24 + k]
        x_recv(20 + k)
        forward_last(20 + k)
        for e in far_first:
            for xx in (_mod(x + 4 - k), _mod(x + k - 3)):
                remote(part.at[pa, xx, _mod(pb + e)], recv2.at[e - 1, xx], s_2, r_2.at[e - 1], along_b(e)).start()
        return u

    lax.fori_loop(0, 4, last_step, 0)
    weights_block(_mod(x - 3 * sx))
    partner_block(3)
    for i in range(24, 28):
        x_recv(i)
    partner_block(4)
    weights_block(_mod(x + 4))
    vp_buf[...] = vp_acc[...].astype(jnp.bfloat16)
    vp_copy = pltpu.make_async_copy(vp_buf, vp_out, s_out.at[8])
    vp_copy.start()

    acc = part[pa, :, pb]
    for e in (1, 7, 2, 6, 3, 5, 4):
        here = recv2.at[e - 1]
        remote(here, here, s_2, r_2.at[e - 1], partner).wait_recv()
        acc += recv2[e - 1]
    s2_buf[:, 0] = acc[:, :4]
    s2_buf[:, 1] = acc[:, 4:]

    for e in far_first:
        for cc in range(2):
            xx = _mod(x + e)
            remote(s2_buf.at[xx, cc], recv3.at[c, e], s_3, r_3.at[c, e], dev(xx, y, z, cc)).start()
    remote(s2_buf.at[x, oc], recv3.at[c, 0], s_3, r_3.at[c, 0], partner).start()

    def got(from_core, e):
        here = recv3.at[from_core, e]
        remote(here, here, s_3, r_3.at[from_core, e], partner).wait_recv()
        return recv3[from_core, e]

    mine, theirs = s2_buf[x, c], got(oc, 0)
    for e in (1, 7, 2, 6, 3, 5, 4):
        mine += got(c, e)
        theirs += got(oc, e)
    mine, theirs = mine / scale, theirs / scale
    wg_buf[:, :256] = jnp.where(c == 0, mine, theirs)
    wg_buf[:, 256:] = jnp.where(c == 0, theirs, mine)
    wg_copy = pltpu.make_async_copy(wg_buf, wg_out, s_out.at[9])
    wg_copy.start()

    c_copy.wait_send()
    z_copy.wait_send()
    remote(z_mine, z_mine, s_zp, r_zp, partner).wait_send()
    mine = a_all.at[pl.ds(0, tok)]
    remote(mine, mine, s_ax, r_ax.at[0], partner).wait_send()
    for sem in (s_r, s_l, s_x, s_p):
        remote(recv_r, recv_r, sem, r_r.at[0], partner).wait_send()
    remote(recv2, recv2, s_2, r_2.at[0], partner).wait_send()
    for there in (recv3.at[0], recv3.at[1, pl.ds(0, 7)]):
        remote(there, there, s_3, r_3.at[0, 0], partner).wait_send()
    for b in range(8):
        at = pl.ds(b * cols, cols)
        pltpu.make_async_copy(ig_buf.at[:, at], ig_out.at[:, at], s_out.at[b]).wait()
    vp_copy.wait()
    wg_copy.wait()


def per_device(activations, value_weight, value_cotangent):
    tok, d = activations.shape
    rows, v = value_weight.shape
    tokens = tok * lax.axis_size("dp") * lax.axis_size("tensor")
    f32, bf16 = jnp.float32, jnp.bfloat16
    dma, vm = pltpu.SemaphoreType.DMA, pltpu.VMEM
    hbm = pl.BlockSpec(memory_space=pl.ANY)
    return pl.pallas_call(
        functools.partial(_kernel, float(tokens) ** 0.5),
        out_shape=(
            jax.ShapeDtypeStruct((tok, v), bf16),
            jax.ShapeDtypeStruct((tok, d), bf16),
            jax.ShapeDtypeStruct((rows * lax.axis_size("tensor") // 1024, v), f32),
        ),
        in_specs=[pl.BlockSpec(memory_space=pltpu.HBM)] * 3,
        out_specs=(hbm,) * 3,
        scratch_shapes=[
            vm((256, 4096), bf16), vm((256, 256), bf16), vm((128, 512), bf16), vm((8, 8, 64, 512), bf16),
            vm((8, 8, 8, 8, 256), f32), vm((ITEMS, 8, 8, 256), f32), vm((ITEMS, 8, 8, 256), f32),
            vm((7, 8, 8, 256), f32), vm((8, 2, 4, 256), f32), vm((2, 8, 4, 256), f32),
            vm((128, 512), f32), vm((128, 512), bf16), vm((128, 4096), bf16), vm((4, 512), f32),
            dma((4,)), dma, dma((8,)), dma, dma, dma, dma, dma, dma,
            dma, dma((ITEMS,)), dma, dma((ITEMS,)), dma, dma((ITEMS,)), dma, dma((4,)),
            dma, dma((7,)), dma, dma((2, 8)), dma((10,)),
        ],
        compiler_params=pltpu.CompilerParams(
            collective_id=0, has_side_effects=True, vmem_limit_bytes=48 * 1024 * 1024
        ),
    )(*(pltpu.with_memory_space_constraint(a, pltpu.HBM) for a in (activations, value_weight.reshape(4, 64, v), value_cotangent)))


def solution(mesh):
    placed = (P(("dp", "tensor"), None), P("tensor", None), P(("dp", "tensor"), None))
    return jax.shard_map(
        per_device,
        mesh=mesh,
        in_specs=placed,
        out_specs=(P(("dp", "tensor"), None), P(("dp", "tensor"), None), P(("tensor", "dp"), None)),
        check_vma=False,
    )
```

time: 86.1 us -> 63.3 us (0.74)
  Pallas kernels: 79.9 us -> 60.3 us
  local copies, waits for them, and re-layouts: 5.3 us -> 2.23 us
    pallas_call x1, Pallas kernels: 79.9 us -> 60.3 us  [per_device(): pl.pallas_call(functools.partial(_kernel, float(tokens) ** 0.5), out_shap...]
    unnamed x9 -> x3, local copies, waits for them, and re-layouts: 5.3 us -> 2.23 us
where the time goes in v2:
time: 63.3 us; the launch traced here: 63.1 us
  Pallas kernels  60.3 us (95%)
  local copies, waits for them, and re-layouts  2.23 us (4%)
  between operations  0.64 us (1%)
    pallas_call x1, Pallas kernels, per_device(): pl.pallas_call(functools.partial(_kernel, float(tokens) ** 0.5), out_shap...  60.3 us
    unnamed x3, local copies, waits for them, and re-layouts  2.23 us

profile of v2, /device:TPU:1, one launch (start us, length us, event | category | flops | bytes accessed | tf_op | source)
XLA Modules:
  0.0 63.1 jit_solution(5928847094053767977)
XLA Ops:
  0.6 60.3 %shard_map.58 = (bf16[128,512]{1,0:T(8,128)(2,1)S(1)}, bf16[128,4096]{1,0:T(8,128)(2,1)S(1)}, f32[4,512]{1,0:T(4,128)S(1)}) custom-call(bf16[128,4096]{1,0:T(8,128)(2,1)} %acts.1, bf16[4,64,512]{2,1,0:T(8,128)(2,1)} %bitcast.1, bf16[128,512]{1,0:T(8,128)(2,1)} %cot.1), custom_call_target="tpu_custom_call" | custom-call | tf_op jit(solution)/shard_map/pallas_call | solution.py:298
  60.9 0.7 %copy.9 = bf16[128,512]{1,0:T(8,128)(2,1)} copy(bf16[128,512]{1,0:T(8,128)(2,1)S(1)} %get-tuple-element.6) | data formatting | bytes 262144
  61.6 1.0 %copy.10 = bf16[128,4096]{1,0:T(8,128)(2,1)} copy(bf16[128,4096]{1,0:T(8,128)(2,1)S(1)} %get-tuple-element.7) | data formatting | bytes 2097152
  62.5 0.6 copy.11

commit v3 on v2

--- a/solution.py
+++ b/solution.py
@@ -156,82 +156,82 @@
             r_copy(2 * k + 1, 3, order(j)).start()
             l_copy(2 * k, 4, order(j)).start()
 
-    def ring_step(p, k):
-        n_even, n_odd = 8 * (p - 1) + 2 * k, 8 * (p - 1) + 2 * k + 1
-        e_r, e_l = 4 - k, k - 3
-        r_copy(n_even, 0, 0).wait_recv()
-        part[_mod(pa + 4 - p), _mod(x + e_r)] += recv_r[n_even]
-        l_copy(n_even, 0, 0).wait_recv()
-        part[_mod(pa - 4 + p), _mod(x + e_l)] += recv_l[n_even]
-        r_copy(n_odd, 0, 0).wait_recv()
-        part[_mod(pa + 3 - p), _mod(x + e_l)] += recv_r[n_odd]
-        l_copy(n_odd, 0, 0).wait_recv()
-        part[_mod(pa - 3 + p), _mod(x + e_r)] += recv_l[n_odd]
-        if p < 3:
-            r_copy(8 * p + 2 * k, 4 - p, e_r).start()
-            l_copy(8 * p + 2 * k, 4 - p, e_l).start()
-            r_copy(8 * p + 2 * k + 1, 3 - p, e_l).start()
-            l_copy(8 * p + 2 * k + 1, 3 - p, e_r).start()
-        else:
-            r_copy(24 + k, 1, e_r).start()
-            l_copy(24 + k, 1, e_l).start()
-
-    def tick(p, forward):
-        def body(k, u):
-            ring_step(p, k)
-            if forward is not None:
-                for h in range(2):
-                    i = 8 * p - 12 + 2 * k + h
-                    x_recv(i)
-                    forward(i)
-            return u
-
-        return body
-
-    def forward(i):
-        x_send(i, i + 8)
-
-    def forward_last(i):
-        @pl.when(c == lax.div(i - 16, 4))
-        def _():
-            x_send(i, 24 + lax.rem(i, 4))
-
-    lax.fori_loop(0, 1, tick(1, None), 0)
     remote(z_mine, z_mine, s_zx, r_zx, z_there).wait_recv()
     remote(z_mine, z_mine, s_zp, r_zp, partner).start()
     x_own(4 + 2 * c)
     x_own(5 + 2 * c)
-    lax.fori_loop(1, 2, tick(1, None), 0)
-    remote(z_other, z_other, s_zp, r_zp, partner).wait_recv()
-    x_own(4 + 2 * oc)
-    x_own(5 + 2 * oc)
-    lax.fori_loop(2, 4, tick(1, forward), 0)
-    loads[3].wait()
-    weights_block(x, first=True)
-    lax.fori_loop(0, 2, tick(2, forward), 0)
-    weights_block(_mod(x - sx))
-    lax.fori_loop(2, 4, tick(2, forward), 0)
-    partner_block(1)
-    lax.fori_loop(0, 2, tick(3, forward), 0)
-    weights_block(_mod(x - 2 * sx))
-    lax.fori_loop(2, 4, tick(3, forward_last), 0)
-    partner_block(2)
+
+    orders = (
+        ((0, 0), (1, 0), (0, 1), (1, 1), (0, 2), (1, 2), (0, 3), (1, 3)),
+        ((0, 0), (0, 1), (1, 0), (0, 2), (1, 1), (0, 3), (1, 2), (1, 3)),
+        ((0, 0), (0, 1), (0, 2), (0, 3), (1, 0), (1, 1), (1, 2), (1, 3)),
+        ((0, 0), (0, 1), (0, 2), (0, 3)),
+    )
+
+    def ring_step(p, pieces):
+        for odd, k in pieces:
+            n = 8 * (p - 1) + orders[p - 1].index((odd, k))
+            to = 4 - p - odd
+            e_r, e_l = (k - 3, 4 - k) if odd else (4 - k, k - 3)
+            r_copy(n, 0, 0).wait_recv()
+            part[_mod(pa + to), _mod(x + e_r)] += recv_r[n]
+            l_copy(n, 0, 0).wait_recv()
+            part[_mod(pa - to), _mod(x + e_l)] += recv_l[n]
+        for odd, k in pieces:
+            to = 4 - p - odd
+            e_r, e_l = (k - 3, 4 - k) if odd else (4 - k, k - 3)
+            if to > 0:
+                n = 8 * p + orders[p].index((odd, k))
+                r_copy(n, to, e_r).start()
+                l_copy(n, to, e_l).start()
+
+    def pass_on(i):
+        x_recv(i)
+        if i < 16:
+            x_send(i, i + 8)
+        elif i < 24:
+
+            @pl.when(c == i // 4 - 4)
+            def _():
+                x_send(i, 24 + i % 4)
+
+    for p in (1, 2, 3):
+        pieces = orders[min(p, 2)]
+        for t in range(4):
+            ring_step(p, pieces[2 * t : 2 * t + 2])
+            if p == 1 and t == 0:
+                remote(z_other, z_other, s_zp, r_zp, partner).wait_recv()
+                x_own(4 + 2 * oc)
+                x_own(5 + 2 * oc)
+            for i in (8 * p - 10 + 2 * t, 8 * p - 9 + 2 * t):
+                if i >= 0:
+                    pass_on(i)
+            if t == 1 and p > 1:
+                weights_block(_mod(x - (p - 1) * sx))
+            if t == 3 and p == 1:
+                loads[3].wait()
+                weights_block(x, first=True)
+            if t == 3 and p > 1:
+                partner_block(p - 1)
 
     far_first = (4, 3, 5, 2, 6, 1, 7)
 
-    def last_step(k, u):
+    for k in range(4):
         r_copy(24 + k, 0, 0).wait_recv()
         part[pa, _mod(x + 4 - k)] += recv_r[24 + k]
         l_copy(24 + k, 0, 0).wait_recv()
         part[pa, _mod(x + k - 3)] += recv_l[24 + k]
-        x_recv(20 + k)
-        forward_last(20 + k)
-        for e in far_first:
-            for xx in (_mod(x + 4 - k), _mod(x + k - 3)):
-                remote(part.at[pa, xx, _mod(pb + e)], recv2.at[e - 1, xx], s_2, r_2.at[e - 1], along_b(e)).start()
-        return u
-
-    lax.fori_loop(0, 4, last_step, 0)
+        for b in range(RING):
+
+            @pl.when(pb != b)
+            def _():
+                e = _mod(b - pb) - 1
+                for xx in (_mod(x + 4 - k), _mod(x + k - 3)):
+                    remote(part.at[pa, xx, b], recv2.at[e, xx], s_2, r_2.at[e], along_b(e + 1)).start()
+
+        if k < 2:
+            pass_on(22 + k)
+
     weights_block(_mod(x - 3 * sx))
     partner_block(3)
     for i in range(24, 28):
@@ -288,6 +288,16 @@
     wg_copy.wait()
 
 
+def _store(vp, ig, wg, vp_out, ig_out, wg_out, sem):
+    rows = ig.shape[0] // 4
+    copies = [pltpu.make_async_copy(ig.at[pl.ds(i * rows, rows)], ig_out.at[pl.ds(i * rows, rows)], sem.at[i]) for i in range(4)]
+    copies += [pltpu.make_async_copy(vp, vp_out, sem.at[4]), pltpu.make_async_copy(wg, wg_out, sem.at[5])]
+    for copy in copies:
+        copy.start()
+    for copy in copies:
+        copy.wait()
+
+
 def per_device(activations, value_weight, value_cotangent):
     tok, d = activations.shape
     rows, v = value_weight.shape
@@ -295,13 +305,14 @@
     f32, bf16 = jnp.float32, jnp.bfloat16
     dma, vm = pltpu.SemaphoreType.DMA, pltpu.VMEM
     hbm = pl.BlockSpec(memory_space=pl.ANY)
-    return pl.pallas_call(
+    shapes = (
+        jax.ShapeDtypeStruct((tok, v), bf16),
+        jax.ShapeDtypeStruct((tok, d), bf16),
+        jax.ShapeDtypeStruct((rows * lax.axis_size("tensor") // 1024, v), f32),
+    )
+    results = pl.pallas_call(
         functools.partial(_kernel, float(tokens) ** 0.5),
-        out_shape=(
-            jax.ShapeDtypeStruct((tok, v), bf16),
-            jax.ShapeDtypeStruct((tok, d), bf16),
-            jax.ShapeDtypeStruct((rows * lax.axis_size("tensor") // 1024, v), f32),
-        ),
+        out_shape=shapes,
         in_specs=[pl.BlockSpec(memory_space=pltpu.HBM)] * 3,
         out_specs=(hbm,) * 3,
         scratch_shapes=[
@@ -317,6 +328,10 @@
             collective_id=0, has_side_effects=True, vmem_limit_bytes=48 * 1024 * 1024
         ),
     )(*(pltpu.with_memory_space_constraint(a, pltpu.HBM) for a in (activations, value_weight.reshape(4, 64, v), value_cotangent)))
+    return pl.pallas_call(
+        _store, out_shape=shapes, in_specs=[hbm] * 3, out_specs=(hbm,) * 3, scratch_shapes=[dma((6,))],
+        compiler_params=pltpu.CompilerParams(vmem_limit_bytes=1024 * 1024),
+    )(*results)
 
 
 def solution(mesh):

time: 63.3 us -> 62.3 us (0.984)
  local copies, waits for them, and re-layouts: 2.23 us -> 0 us
  Pallas kernels: 60.3 us -> 61.6 us
    unnamed x3 -> x0, local copies, waits for them, and re-layouts: 2.23 us -> none
    pallas_call x0 -> x1, Pallas kernels: none -> 1.06 us  [per_device(): pl.pallas_call(_store, out_shape=shapes, in_specs=[hbm] * 3, out_specs=(h...]
where the time goes in v3:
time: 62.3 us; the launch traced here: 62.2 us
  Pallas kernels  61.6 us (99%)
  between operations  0.64 us (1%)
    pallas_call x1, Pallas kernels, per_device(): pl.pallas_call(functools.partial(_kernel, float(tokens) ** 0.5), out_shap...  60.5 us

profile of v3, /device:TPU:1, one launch (start us, length us, event | category | flops | bytes accessed | tf_op | source)
XLA Modules:
  0.0 62.2 jit_solution(13927622498326998499)
XLA Ops:
  0.6 60.5 %shard_map.58 = (bf16[128,512]{1,0:T(8,128)(2,1)S(1)}, bf16[128,4096]{1,0:T(8,128)(2,1)S(1)}, f32[4,512]{1,0:T(4,128)S(1)}) custom-call(bf16[128,4096]{1,0:T(8,128)(2,1)} %acts.1, bf16[4,64,512]{2,1,0:T(8,128)(2,1)} %bitcast.1, bf16[128,512]{1,0:T(8,128)(2,1)} %cot.1), custom_call_target="tpu_custom_call" | custom-call | tf_op jit(solution)/shard_map/pallas_call | solution.py:313
  61.1 1.1 %shard_map.59 = (bf16[128,512]{1,0:T(8,128)(2,1)}, bf16[128,4096]{1,0:T(8,128)(2,1)}, f32[4,512]{1,0:T(4,128)}) custom-call(bf16[128,512]{1,0:T(8,128)(2,1)S(1)} %get-tuple-element.6.vp, bf16[128,4096]{1,0:T(8,128)(2,1)S(1)} %get-tuple-element.7.ig, f32[4,512]{1,0:T(4,128)S(1)} %get-tuple-element.8.wg), custom_call_target="tpu_custom_call" | custom-call | tf_op jit(solution)/shard_map/pallas_call | solution.py:331

commit v4 on v3

--- a/solution.py
+++ b/solution.py
@@ -18,9 +18,11 @@
 
 def _kernel(scale, acts, w, cot, vp_out, ig_out, wg_out,
             a_all, c_pair, c_own, w_all, part, recv_r, recv_l, recv2, s2_buf, recv3,
+            recvx_r, recvx_l, recv4, v_buf, recv5,
             vp_acc, vp_buf, ig_buf, wg_buf,
             s_load, s_ax, r_ax, s_cx, r_cx, s_zx, r_zx, s_zp, r_zp,
-            s_r, r_r, s_l, r_l, s_x, r_x, s_p, r_p, s_2, r_2, s_3, r_3, s_out):
+            s_r, r_r, s_l, r_l, s_x, r_x, s_p, r_p, s_2, r_2, s_3, r_3,
+            s_xr, r_xr, s_xl, r_xl, s_4, r_4, s_5, r_5, s_out):
     dp, tn = lax.axis_index("dp"), lax.axis_index("tensor")
     c, y, zh = lax.rem(dp, 2), lax.rem(lax.div(dp, 2), RING), lax.div(dp, 2 * RING)
     x, zl = lax.div(tn, 2), lax.rem(tn, 2)
@@ -36,8 +38,8 @@
     def along_a(step):
         return dev(x, _mod(y + step * oc), _mod(z + step * c), c)
 
-    def along_b(step):
-        return dev(x, _mod(y + step * c), _mod(z + step * oc), c)
+    def along_b(step, core=None):
+        return dev(x, _mod(y + step * c), _mod(z + step * oc), c if core is None else core)
 
     def along_x(step):
         return dev(_mod(x + step), y, z, c)
@@ -127,12 +129,36 @@
             weights_block(_mod(x + sx * p))
 
     right, left = along_a(1), along_a(-1)
+    near, far = pl.ds(0, 7), 7
+    slots = [_mod(v - pb + 3) for v in range(8)]
+    x_right, x_left = along_x(1), along_x(-1)
+
+    def xr_copy(n):
+        src = part.at[pl.ds(n % 2 * 4, 4), _mod(x + 4 - (n + 1) // 2), far]
+        return remote(src, recvx_r.at[n], s_xr, r_xr.at[n], x_right)
+
+    def xl_copy(n):
+        src = part.at[pl.ds((n + 1) % 2 * 4, 4), _mod(x - 4 + (n + 1) // 2), far]
+        return remote(src, recvx_l.at[n], s_xl, r_xl.at[n], x_left)
+
+    def x_step(items):
+        for n in items:
+            to = 3 - (n + 1) // 2
+            xr_copy(n).wait_recv()
+            part[n % 2 * 4 : n % 2 * 4 + 4, _mod(x + to), far] += recvx_r[n]
+            h = (n + 1) % 2 * 4
+            xl_copy(n).wait_recv()
+            part[h : h + 4, _mod(x - to), far] += recvx_l[n]
+        for n in items:
+            if n + 2 < 7:
+                xr_copy(n + 2).start()
+                xl_copy(n + 2).start()
 
     def r_copy(n, to, xx):
-        return remote(part.at[_mod(pa + to), _mod(x + xx)], recv_r.at[n], s_r, r_r.at[n], right)
+        return remote(part.at[_mod(pa + to), _mod(x + xx), near], recv_r.at[n], s_r, r_r.at[n], right)
 
     def l_copy(n, to, xx):
-        return remote(part.at[_mod(pa - to), _mod(x + xx)], recv_l.at[n], s_l, r_l.at[n], left)
+        return remote(part.at[_mod(pa - to), _mod(x + xx), near], recv_l.at[n], s_l, r_l.at[n], left)
 
     for load in loads[:3]:
         load.wait()
@@ -148,13 +174,16 @@
         for zz in range(8):
             base = (zz % 2) * 256 + (zz // 2) * 64
             for yy in range(8):
-                part[yy * oc + zz * c, xb, zz * oc + yy * c] = prod[base + yy * 8 : base + yy * 8 + 8]
+                part[yy * oc + zz * c, xb, slots[zz] * oc + slots[yy] * c] = prod[base + yy * 8 : base + yy * 8 + 8]
         if j % 2 == 0:
             r_copy(2 * k, 4, order(j)).start()
             l_copy(2 * k + 1, 3, order(j)).start()
         else:
             r_copy(2 * k + 1, 3, order(j)).start()
             l_copy(2 * k, 4, order(j)).start()
+        if j in (0, 2):
+            xr_copy(j // 2).start()
+            xl_copy(j // 2).start()
 
     remote(z_mine, z_mine, s_zx, r_zx, z_there).wait_recv()
     remote(z_mine, z_mine, s_zp, r_zp, partner).start()
@@ -174,9 +203,9 @@
             to = 4 - p - odd
             e_r, e_l = (k - 3, 4 - k) if odd else (4 - k, k - 3)
             r_copy(n, 0, 0).wait_recv()
-            part[_mod(pa + to), _mod(x + e_r)] += recv_r[n]
+            part[_mod(pa + to), _mod(x + e_r), 0:7] += recv_r[n]
             l_copy(n, 0, 0).wait_recv()
-            part[_mod(pa - to), _mod(x + e_l)] += recv_l[n]
+            part[_mod(pa - to), _mod(x + e_l), 0:7] += recv_l[n]
         for odd, k in pieces:
             to = 4 - p - odd
             e_r, e_l = (k - 3, 4 - k) if odd else (4 - k, k - 3)
@@ -203,9 +232,11 @@
                 remote(z_other, z_other, s_zp, r_zp, partner).wait_recv()
                 x_own(4 + 2 * oc)
                 x_own(5 + 2 * oc)
-            for i in (8 * p - 10 + 2 * t, 8 * p - 9 + 2 * t):
+            for i in (8 * p - 12 + 2 * t, 8 * p - 11 + 2 * t):
                 if i >= 0:
                     pass_on(i)
+            if t == 1:
+                x_step((2 * p - 2, 2 * p - 1))
             if t == 1 and p > 1:
                 weights_block(_mod(x - (p - 1) * sx))
             if t == 3 and p == 1:
@@ -218,21 +249,42 @@
 
     for k in range(4):
         r_copy(24 + k, 0, 0).wait_recv()
-        part[pa, _mod(x + 4 - k)] += recv_r[24 + k]
+        part[pa, _mod(x + 4 - k), 0:7] += recv_r[24 + k]
         l_copy(24 + k, 0, 0).wait_recv()
-        part[pa, _mod(x + k - 3)] += recv_l[24 + k]
-        for b in range(RING):
-
-            @pl.when(pb != b)
-            def _():
-                e = _mod(b - pb) - 1
-                for xx in (_mod(x + 4 - k), _mod(x + k - 3)):
-                    remote(part.at[pa, xx, b], recv2.at[e, xx], s_2, r_2.at[e], along_b(e + 1)).start()
-
-        if k < 2:
-            pass_on(22 + k)
-
+        part[pa, _mod(x + k - 3), 0:7] += recv_l[24 + k]
+        for e in (3, -3, 2, -2, 1, -1):
+            for xx in (_mod(x + 4 - k), _mod(x + k - 3)):
+                remote(part.at[pa, xx, e + 3], recv2.at[e + 3, xx], s_2, r_2.at[e + 3], along_b(e)).start()
+        pass_on(20 + k)
+
+    x_step((6,))
+    for e in far_first:
+        remote(part.at[_mod(pa + e), x, far], recv4.at[e - 1], s_4, r_4.at[e - 1], along_a(e)).start()
     weights_block(_mod(x - 3 * sx))
+    val = part[pa, x, far]
+    for e in (1, 7, 2, 6, 3, 5, 4):
+        here = recv4.at[e - 1]
+        remote(here, here, s_4, r_4.at[e - 1], partner).wait_recv()
+        val += recv4[e - 1]
+    v_buf[0] = val[:4]
+    v_buf[1] = val[4:]
+    for cc in range(2):
+        remote(v_buf.at[cc], recv5.at[c], s_5, r_5.at[c], along_b(4, cc)).start()
+
+    acc = part[pa, :, 3]
+    for e in (-1, 1, -2, 2, -3, 3):
+        here = recv2.at[e + 3]
+        remote(here, here, s_2, r_2.at[e + 3], partner).wait_recv()
+        acc += recv2[e + 3]
+    s2_buf[:, 0] = acc[:, :4]
+    s2_buf[:, 1] = acc[:, 4:]
+
+    for e in far_first:
+        for cc in range(2):
+            xx = _mod(x + e)
+            remote(s2_buf.at[xx, cc], recv3.at[c, e], s_3, r_3.at[c, e], dev(xx, y, z, cc)).start()
+    remote(s2_buf.at[x, oc], recv3.at[c, 0], s_3, r_3.at[c, 0], partner).start()
+
     partner_block(3)
     for i in range(24, 28):
         x_recv(i)
@@ -242,20 +294,6 @@
     vp_copy = pltpu.make_async_copy(vp_buf, vp_out, s_out.at[8])
     vp_copy.start()
 
-    acc = part[pa, :, pb]
-    for e in (1, 7, 2, 6, 3, 5, 4):
-        here = recv2.at[e - 1]
-        remote(here, here, s_2, r_2.at[e - 1], partner).wait_recv()
-        acc += recv2[e - 1]
-    s2_buf[:, 0] = acc[:, :4]
-    s2_buf[:, 1] = acc[:, 4:]
-
-    for e in far_first:
-        for cc in range(2):
-            xx = _mod(x + e)
-            remote(s2_buf.at[xx, cc], recv3.at[c, e], s_3, r_3.at[c, e], dev(xx, y, z, cc)).start()
-    remote(s2_buf.at[x, oc], recv3.at[c, 0], s_3, r_3.at[c, 0], partner).start()
-
     def got(from_core, e):
         here = recv3.at[from_core, e]
         remote(here, here, s_3, r_3.at[from_core, e], partner).wait_recv()
@@ -265,7 +303,10 @@
     for e in (1, 7, 2, 6, 3, 5, 4):
         mine += got(c, e)
         theirs += got(oc, e)
-    mine, theirs = mine / scale, theirs / scale
+    for core in range(2):
+        here = recv5.at[core]
+        remote(here, here, s_5, r_5.at[core], partner).wait_recv()
+    mine, theirs = (mine + recv5[c]) / scale, (theirs + recv5[oc]) / scale
     wg_buf[:, :256] = jnp.where(c == 0, mine, theirs)
     wg_buf[:, 256:] = jnp.where(c == 0, theirs, mine)
     wg_copy = pltpu.make_async_copy(wg_buf, wg_out, s_out.at[9])
@@ -276,9 +317,13 @@
     remote(z_mine, z_mine, s_zp, r_zp, partner).wait_send()
     mine = a_all.at[pl.ds(0, tok)]
     remote(mine, mine, s_ax, r_ax.at[0], partner).wait_send()
-    for sem in (s_r, s_l, s_x, s_p):
+    for sem in (s_r, s_l):
         remote(recv_r, recv_r, sem, r_r.at[0], partner).wait_send()
-    remote(recv2, recv2, s_2, r_2.at[0], partner).wait_send()
+    for sem in (s_x, s_p):
+        for there in (w_all.at[pl.ds(0, 3)], w_all.at[0, pl.ds(0, 4)]):
+            remote(there, there, sem, r_r.at[0], partner).wait_send()
+    for there, sem in ((recv2.at[pl.ds(0, 6)], s_2), (recvx_r, s_xr), (recvx_l, s_xl), (recv4, s_4), (recv5, s_5)):
+        remote(there, there, sem, r_r.at[0], partner).wait_send()
     for there in (recv3.at[0], recv3.at[1, pl.ds(0, 7)]):
         remote(there, there, s_3, r_3.at[0, 0], partner).wait_send()
     for b in range(8):
@@ -317,12 +362,14 @@
         out_specs=(hbm,) * 3,
         scratch_shapes=[
             vm((256, 4096), bf16), vm((256, 256), bf16), vm((128, 512), bf16), vm((8, 8, 64, 512), bf16),
-            vm((8, 8, 8, 8, 256), f32), vm((ITEMS, 8, 8, 256), f32), vm((ITEMS, 8, 8, 256), f32),
+            vm((8, 8, 8, 8, 256), f32), vm((ITEMS, 7, 8, 256), f32), vm((ITEMS, 7, 8, 256), f32),
             vm((7, 8, 8, 256), f32), vm((8, 2, 4, 256), f32), vm((2, 8, 4, 256), f32),
+            vm((7, 4, 8, 256), f32), vm((7, 4, 8, 256), f32), vm((7, 8, 256), f32), vm((2, 4, 256), f32), vm((2, 4, 256), f32),
             vm((128, 512), f32), vm((128, 512), bf16), vm((128, 4096), bf16), vm((4, 512), f32),
             dma((4,)), dma, dma((8,)), dma, dma, dma, dma, dma, dma,
             dma, dma((ITEMS,)), dma, dma((ITEMS,)), dma, dma((ITEMS,)), dma, dma((4,)),
-            dma, dma((7,)), dma, dma((2, 8)), dma((10,)),
+            dma, dma((7,)), dma, dma((2, 8)),
+            dma, dma((7,)), dma, dma((7,)), dma, dma((7,)), dma, dma((2,)), dma((10,)),
         ],
         compiler_params=pltpu.CompilerParams(
             collective_id=0, has_side_effects=True, vmem_limit_bytes=48 * 1024 * 1024

time: 62.3 us -> 60.9 us (0.978)
  Pallas kernels: 61.6 us -> 60.2 us
    pallas_call x1, Pallas kernels: 60.5 us -> 59.1 us  [per_device(): pl.pallas_call(functools.partial(_kernel, float(tokens) ** 0.5), out_shap...]
where the time goes in v4:
time: 60.9 us; the launch traced here: 60.8 us
  Pallas kernels  60.2 us (99%)
  between operations  0.64 us (1%)
    pallas_call x1, Pallas kernels, per_device(): pl.pallas_call(functools.partial(_kernel, float(tokens) ** 0.5), out_shap...  59.1 us

profile of v4, /device:TPU:1, one launch (start us, length us, event | category | flops | bytes accessed | tf_op | source)
XLA Modules:
  0.0 60.8 jit_solution(15742942626109119179)
XLA Ops:
  0.6 59.1 %shard_map.58 = (bf16[128,512]{1,0:T(8,128)(2,1)S(1)}, bf16[128,4096]{1,0:T(8,128)(2,1)S(1)}, f32[4,512]{1,0:T(4,128)S(1)}) custom-call(bf16[128,4096]{1,0:T(8,128)(2,1)} %acts.1, bf16[4,64,512]{2,1,0:T(8,128)(2,1)} %bitcast.1, bf16[128,512]{1,0:T(8,128)(2,1)} %cot.1), custom_call_target="tpu_custom_call" | custom-call | tf_op jit(solution)/shard_map/pallas_call | solution.py:358
  59.7 1.1 %shard_map.59 = (bf16[128,512]{1,0:T(8,128)(2,1)}, bf16[128,4096]{1,0:T(8,128)(2,1)}, f32[4,512]{1,0:T(4,128)}) custom-call(bf16[128,512]{1,0:T(8,128)(2,1)S(1)} %get-tuple-element.6.vp, bf16[128,4096]{1,0:T(8,128)(2,1)S(1)} %get-tuple-element.7.ig, f32[4,512]{1,0:T(4,128)S(1)} %get-tuple-element.8.wg), custom_call_target="tpu_custom_call" | custom-call | tf_op jit(solution)/shard_map/pallas_call | solution.py:378
